TPU v7x, 32 devices: a whole 2x2x4 slice. The times are simulated.
32 devices in a mesh: row: 4 (over z), col: 8 (over y, x, core).
Axes of the slice: x: 2, y: 2, z: 4, core: 2. Of those that a mesh axis runs over, the one named last changes fastest.
Arguments:
- gradient: bfloat16 [28672, 8192], P('row', 'col'), may hold values from -6 to 6
- projector: bfloat16 [8192, 1024], P('col', 'row'), may hold values from -0.0625 to 0.0625
- first_moment: float32 [1024, 28672], P('col', 'row'), may hold values from -2 to 2
- second_moment: float32 [1024, 28672], P('col', 'row'), may hold values from 0.0001 to 0.01
Outputs:
- update: float32 [28672, 8192], P('row', 'col')
- first_next: float32 [1024, 28672], P('col', 'row')
- second_next: float32 [1024, 28672], P('col', 'row')
All inputs are finite; a program needn't handle non-finite values.
Results may differ from a plain program's by a relative error of at most 0.0058.
Values may be sent and summed in bfloat16 or wider, within the bound.
A program may use at most 128 MiB of HBM per device.

v0:
```python
import jax
import jax.numpy as jnp
from jax import lax
from jax.sharding import PartitionSpec as P


def adam_moments(compressed, first_moment, second_moment):
    first_next = 0.9 * first_moment + 0.1 * compressed
    second_next = 0.999 * second_moment + 0.001 * compressed * compressed
    corr_first = 1.0 - 0.9**10
    corr_second = 1.0 - 0.999**10
    direction = (first_next / corr_first / (jnp.sqrt(second_next / corr_second) + 1e-08)).astype(
        jnp.bfloat16
    )
    return (direction, first_next, second_next)


def shards(gradient, projector, first_moment, second_moment):
    proj_rows = lax.all_gather(projector, "row", axis=1, tiled=True)
    proj_part = proj_rows
    compressed = lax.psum_scatter(
        lax.dot_general(
            proj_part, gradient, (((0,), (1,)), ((), ())), preferred_element_type=jnp.float32
        ),
        "col",
        scatter_dimension=0,
        tiled=True,
    )
    direction, first_next, second_next = adam_moments(compressed, first_moment, second_moment)
    proj_part = proj_rows
    update = lax.dot_general(
        lax.all_gather(direction, "col", axis=0, tiled=True),
        proj_part,
        (((0,), (1,)), ((), ())),
        preferred_element_type=jnp.float32,
    )
    return (update, first_next, second_next)


def solution(mesh):
    return jax.shard_map(
        shards,
        mesh=mesh,
        in_specs=(P("row", "col"), P("col", "row"), P("col", "row"), P("col", "row")),
        out_specs=(P("row", "col"), P("col", "row"), P("col", "row")),
        check_vma=False,
    )
```

profile of v0, /device:TPU:0, one launch (start us, length us, event | category | flops | bytes accessed | tf_op | source)
XLA Modules:
  0.0 382.0 jit_solution(16428423400285299975)
XLA Ops:
  7.2 0.0 all-gather.3.cloned.1.call-start
  7.2 0.7 all-gather.3.cloned.1.call-update
  7.9 0.0 reduce-scatter.2.cloned.1.call-start
  7.9 50.6 %all-gather.3.cloned.1.call-done = bf16[1024,1024]{1,0:T(8,128)(2,1)} async-done(((bf16[1024,256]{1,0:T(8,128)(2,1)}), bf16[1024,1024]{1,0:T(8,128)(2,1)}) %all-gather.3.cloned.1.call-update) | async-done | bytes 2097168 | tf_op jit(solution)/shard_map/all_gather | solution.py:19
  58.5 24.8 %fusion.2 = f32[1024,7168]{1,0:T(8,128)} fusion(bf16[1024,1024]{1,0:T(8,128)(2,1)} %all-gather.3.cloned.1.call-done, bf16[7168,1024]{1,0:T(8,128)(2,1)} %param.4), kind=kOutput, calls=%fused_computation.4 | convolution fusion | flops 15032385536 | bytes 46137344 | tf_op jit(solution)/shard_map/dot_general | solution.py:22
  83.3 0.0 reduce-scatter.2.cloned.1.call-update
  83.3 0.0 copy-start
  83.3 0.2 all-gather.5.cloned.1.call-start
  83.6 179.1 %reduce-scatter.2.cloned.1.call-done = f32[128,7168]{1,0:T(8,128)} async-done(((f32[1024,7168]{1,0:T(8,128)}), f32[128,7168]{1,0:T(8,128)}) %reduce-scatter.2.cloned.1.call-update) | async-done | bytes 3670032 | tf_op jit(solution)/shard_map/reduce_scatter | solution.py:21
  262.6 7.5 %divide_convert_fusion = (bf16[128,7168]{1,0:T(8,128)(2,1)}, f32[128,7168]{1,0:T(8,128)}, f32[128,7168]{1,0:T(8,128)}) fusion(f32[128,7168]{1,0:T(8,128)} %reduce-scatter.2.cloned.1.call-done, f32[128,7168]{1,0:T(8,128)} %param.6, f32[128,7168]{1,0:T(8,128)} %param.7), kind=kLoop, calls=%fused_computation.2 | loop fusion | flops 11010048 | bytes 20185088 | tf_op jit(solution)/shard_map/convert_element_type | solution.py:12
  270.2 0.0 all-gather.5.cloned.1.call-update
  270.2 81.0 %all-gather.5.cloned.1.call-done = bf16[1024,7168]{1,0:T(8,128)(2,1)} async-done(((bf16[128,7168]{1,0:T(8,128)(2,1)}), bf16[1024,7168]{1,0:T(8,128)(2,1)}) %all-gather.5.cloned.1.call-update) | async-done | bytes 14680080 | tf_op jit(solution)/shard_map/all_gather | solution.py:32
  351.2 0.0 copy-done
  351.2 24.3 %fusion.3 = f32[7168,1024]{1,0:T(8,128)} fusion(bf16[1024,7168]{1,0:T(8,128)(2,1)} %all-gather.5.cloned.1.call-done, bf16[1024,1024]{1,0:T(8,128)(2,1)S(1)} %copy-done), kind=kOutput, calls=%fused_computation.5 | convolution fusion | flops 15032385536 | bytes 46137344 | tf_op jit(solution)/shard_map/dot_general | solution.py:31
Async XLA Ops:
  7.2 51.4 %all-gather.3.cloned.1.call-start = ((), (), s32[]{:S(2)}) async-start(), calls=%async_computation.1 | async-start | bytes 2621440 | tf_op jit(solution)/shard_map/all_gather | solution.py:19
  7.9 254.7 %reduce-scatter.2.cloned.1.call-start = ((), (), s32[]{:S(2)}) async-start(), calls=%async_computation.2 | async-start | bytes 33030144 | tf_op jit(solution)/shard_map/reduce_scatter | solution.py:21
  83.3 267.9 %copy-start = (bf16[1024,1024]{1,0:T(8,128)(2,1)S(1)}, bf16[1024,1024]{1,0:T(8,128)(2,1)}, u32[]{:S(2)}) copy-start(bf16[1024,1024]{1,0:T(8,128)(2,1)} %all-gather.3.cloned.1.call-done) | copy-start | bytes 6291460
  83.3 267.9 %all-gather.5.cloned.1.call-start = ((), (), s32[]{:S(2)}) async-start(), calls=%async_computation.3 | async-start | bytes 16515072 | tf_op jit(solution)/shard_map/all_gather | solution.py:32
Sparse Core Ops, SparseCore 0:
  9.5 48.9 all-gather.2
  83.5 179.1 reduce-scatter.1
  270.3 80.8 all-gather.4
where the time goes:
time: 382 us
  waiting for transfers between devices  311 us (81%)
  matrix products  49.1 us (13%)
  between operations  13.8 us (4%)
  other arithmetic  7.53 us (2%)
    reduce_scatter x1, waiting for transfers between devices, shards(): lax.psum_scatter(lax.dot_general(proj_part, gradient, (((0,), (1,)), ((),...  179 us
    all_gather x1, waiting for transfers between devices, shards(): lax.all_gather(direction, 'col', axis=0, tiled=True)  81 us
    all_gather x1, waiting for transfers between devices, shards(): proj_rows = lax.all_gather(projector, 'row', axis=1, tiled=True)  50.6 us
    dot_general x1, matrix products, shards(): lax.dot_general(proj_part, gradient, (((0,), (1,)), ((), ())), preferred_...  24.8 us
    dot_general x1, matrix products, shards(): lax.dot_general(lax.all_gather(direction, 'col', axis=0, tiled=True), pro...  24.3 us
  transfers between devices with their start and end apart: 3, of which 3 were waited for; matrix products, arithmetic and copies ran while one was open for 0% of the time, Pallas kernels for 0%

commit v1 on v0

v1 whole, which is shorter than its diff:
```python
import functools
import math

import jax
import jax.numpy as jnp
from jax import lax
from jax.experimental import pallas as pl
from jax.experimental.pallas import tpu as pltpu
from jax.sharding import PartitionSpec as P


SHARES = (1, 1, 1, 1)
BF16, F32 = jnp.bfloat16, jnp.float32


def swap(x, bit, n):
    return lax.ppermute(x, "col", [(i, i ^ (1 << bit)) for i in range(n)])


def shift(x, by, n):
    return lax.ppermute(x, "row", [(i, (i + by) % n) for i in range(n)])


def gather_rows(shard, n):
    if n == 1:
        return [shard]
    if n == 2:
        return [shard, shift(shard, 1, n)]
    found = {0: shard}
    up = down = shard
    for d in range(1, (n + 1) // 2):
        up, down = shift(up, 1, n), shift(down, -1, n)
        found[d], found[n - d] = up, down
    if n % 2 == 0:
        half = shard.shape[0] // 2
        found[n // 2] = jnp.concatenate([shift(up[:half], 1, n), shift(down[half:], -1, n)])
    return [found[d] for d in range(n)]


VMEM = pltpu.MemorySpace.VMEM


def pick_body(rows, parts, *refs):
    where, shards, outs, full = refs[0], refs[1 : parts + 1], refs[parts + 1 : -1], refs[-1]
    height = full.shape[0] // parts
    for d, shard in enumerate(shards):
        full[d * height : (d + 1) * height] = shard[...]
    for k, out in enumerate(outs):
        for p in range(out.shape[0] // rows):
            start = pl.multiple_of(where[k, p] * rows, rows)
            out[p * rows : (p + 1) * rows] = full[pl.ds(start, rows)]


def pick_blocks(found, where, rows):
    shape = (len(found) * found[0].shape[0], found[0].shape[1])
    turns = where.shape[0]
    return pl.pallas_call(
        functools.partial(pick_body, rows, len(found)),
        out_shape=[jax.ShapeDtypeStruct(shape, BF16)] * turns,
        in_specs=[pl.BlockSpec(memory_space=pltpu.MemorySpace.SMEM)]
        + [pl.BlockSpec(memory_space=VMEM)] * len(found),
        out_specs=[pl.BlockSpec(memory_space=VMEM)] * turns,
        scratch_shapes=[pltpu.VMEM(shape, BF16)],
        name="pick",
    )(where, *found)


def tile(*extents):
    return next(t for t in (1024, 896, 512, 256, 128) if math.gcd(*extents) % t == 0)


def cut(rows):
    unit = 512 if rows % (512 * sum(SHARES)) == 0 else 128
    edges = [0]
    for k in range(len(SHARES)):
        edges.append(rows * sum(SHARES[: k + 1]) // sum(SHARES) // unit * unit)
    return [(a, b - a) for a, b in zip(edges, edges[1:]) if b > a]


def adam_body(parts, *refs):
    terms, (first, second) = refs[:parts], refs[parts : parts + 2]
    direction, first_next, second_next = refs[-3:]
    c = terms[0][...].astype(F32)
    for t in terms[1:]:
        c = c + t[...].astype(F32)
    f = 0.9 * first[...] + 0.1 * c
    s = 0.999 * second[...] + 0.001 * c * c
    corr_first = 1.0 - 0.9**10
    corr_second = 1.0 - 0.999**10
    direction[...] = (f / corr_first / (jnp.sqrt(s / corr_second) + 1e-08)).astype(BF16)
    first_next[...] = f
    second_next[...] = s


def adam(offset, terms, first, second, moments):
    rows, cols = first.shape
    m = terms[0].shape[1]
    t = tile(m, offset)
    at = lambda i: (0, offset // t + i)
    last = lambda x: pl.BlockSpec((rows, t), functools.partial(lambda r, i: (r, i), x.shape[0] // rows - 1))
    whole = pl.BlockSpec((rows, t), at)
    anywhere = [pl.BlockSpec(memory_space=pl.ANY)] * len(moments)
    n = len(terms)
    return pl.pallas_call(
        functools.partial(adam_body, n),
        grid=(m // t,),
        out_shape=(
            jax.ShapeDtypeStruct((rows, m), BF16),
            jax.ShapeDtypeStruct((rows, cols), F32),
            jax.ShapeDtypeStruct((rows, cols), F32),
        ),
        in_specs=[last(x) for x in terms] + [whole, whole] + anywhere,
        out_specs=(pl.BlockSpec((rows, t), lambda i: (0, i)), whole, whole),
        input_output_aliases={n + 2: 1, n + 3: 2} if moments else {},
        cost_estimate=pl.CostEstimate(
            flops=20 * rows * m, bytes_accessed=rows * m * 24, transcendentals=2 * rows * m
        ),
        name="adam",
    )(*terms, first, second, *moments)


def back_body(parts, *refs):
    pieces, proj, out = refs[:parts], refs[parts], refs[-1]
    t = out.shape[0]
    at = pl.ds(pl.multiple_of(pl.program_id(0) * t, t), t)
    whole = jnp.concatenate([p[:, at] for p in pieces], axis=0)
    out[...] = lax.dot_general(whole, proj[...], (((0,), (0,)), ((), ())), preferred_element_type=F32)


def back(offset, pieces, proj, total, update):
    m = pieces[0].shape[1]
    ranks, width = proj.shape
    t = tile(m, offset)
    n = len(pieces)
    return pl.pallas_call(
        functools.partial(back_body, n),
        grid=(m // t,),
        out_shape=jax.ShapeDtypeStruct((total, width), F32),
        in_specs=[pl.BlockSpec(memory_space=VMEM)] * (n + 1)
        + [pl.BlockSpec(memory_space=pl.ANY)] * len(update),
        out_specs=pl.BlockSpec((t, width), lambda i: (offset // t + i, 0)),
        input_output_aliases={n + 1: 0} if update else {},
        cost_estimate=pl.CostEstimate(
            flops=2 * m * ranks * width, bytes_accessed=m * (2 * ranks + 4 * width), transcendentals=0
        ),
        name="back",
    )(*pieces, proj, *update)


def project(proj, grad):
    return lax.dot_general(proj, grad, (((1,), (1,)), ((), ())), preferred_element_type=F32)


def shards(n_row, n_col, gradient, projector, first_moment, second_moment):
    levels = n_col.bit_length() - 1
    own = first_moment.shape[0]
    ranks = own * n_col
    rows = gradient.shape[0]
    row, col = lax.axis_index("row"), lax.axis_index("col")

    found = gather_rows(projector.T, n_row)
    per_row = n_col // n_row
    orders, order = [], []
    for turn in range(2):
        bits = list(range(levels))
        if turn and levels > 1:
            bits = [0] + bits[:0:-1]
        away = []
        for p in range(n_col):
            digits = [(p >> (levels - 1 - k)) & 1 for k in range(levels)]
            away.append(sum((1 << b) for b, d in zip(bits, digits) if d == 0))
        owner = col ^ jnp.array(away, jnp.int32)
        order.append(lax.rem(row - owner // per_row + n_row, n_row) * per_row + owner % per_row)
        orders.append(bits)
    projs = list(pick_blocks(found, jnp.stack(order), own))

    update, moments = (), ()
    second = []
    for c, (offset, m) in enumerate(cut(rows)):
        bits, proj = orders[c % 2], projs[c % 2]
        if c == 2:
            proj, projs[1], *_ = lax.optimization_barrier((proj, projs[1], *second))
        grad = gradient[offset : offset + m]
        starts = [ranks - (ranks >> k) for k in range(levels + 1)]
        deep = min(2, levels)
        got = []
        rest = None
        for k in range(levels):
            a, b = starts[k], starts[k + 1]
            if k < deep:
                piece = project(proj[a:b], grad)
            else:
                if rest is None:
                    rest = project(proj[starts[deep] :], grad).astype(BF16)
                piece = rest[a - starts[deep] : b - starts[deep]].astype(F32)
            for j, r in enumerate(got):
                piece = piece + r[a - starts[j + 1] : b - starts[j + 1]].astype(F32)
            sent = piece.astype(BF16)
            if k == 1:
                second.append(sent)
            got.append(swap(sent, bits[k], n_col))
        if rest is None:
            rest = project(proj[starts[deep] :], grad)
        direction, *moments = adam(offset, [rest, *got], first_moment, second_moment, moments)
        held = [direction]
        for k in reversed(range(levels)):
            if k:
                whole = held[0] if len(held) == 1 else jnp.concatenate(held)
                held = [swap(whole, bits[k], n_col), whole]
            else:
                held = [swap(x, bits[k], n_col) for x in held] + held
        update = (back(offset, held, proj, rows, update),)
    return (update[0], *moments)


def solution(mesh):
    def step(*args):
        return shards(mesh.shape["row"], mesh.shape["col"], *args)

    return jax.shard_map(
        step,
        mesh=mesh,
        in_specs=(P("row", "col"), P("col", "row"), P("col", "row"), P("col", "row")),
        out_specs=(P("row", "col"), P("col", "row"), P("col", "row")),
        check_vma=False,
    )
```

time: 382 us -> 239 us (0.63)
  waiting for transfers between devices: 311 us -> 113 us
  Pallas kernels: 0 us -> 52.6 us
  starting transfers between devices: 0.3 us -> 26.9 us
  matrix products: 49.1 us -> 31.2 us
  between operations: 13.8 us -> 1 us
  local copies, waits for them, and re-layouts: 0.01 us -> 8.72 us
    reduce_scatter x1 -> x0, waiting for transfers between devices: 179 us -> none  [shards(): lax.psum_scatter(lax.dot_general(proj_part, gradient, (((0,), (1,)), ((),...]
    all_gather x2 -> x0, waiting for transfers between devices: 132 us -> none  [the longest x1 81 us: shards(): lax.all_gather(direction, 'col', axis=0, tiled=True)]
    ppermute x0 -> x32, waiting for transfers between devices: none -> 113 us  [the longest x28 83.1 us: swap(): return lax.ppermute(x, 'col', [(i, i ^ 1 << bit) for i in range(n)])]
    pallas_call x0 -> x9, Pallas kernels: none -> 52.6 us  [the longest x4 35.1 us: back(): pl.pallas_call(functools.partial(back_body, n), grid=(m // t,), out_shape...]
    ppermute x0 -> x32, starting transfers between devices: none -> 26.9 us  [the longest x28 18.6 us: swap(): return lax.ppermute(x, 'col', [(i, i ^ 1 << bit) for i in range(n)])]
    dot_general x2 -> x12, matrix products: 49.1 us -> 31.2 us  [project(): lax.dot_general(proj, grad, (((1,), (1,)), ((), ())), preferred_element_t...]
    unnamed x2 -> x55, local copies, waits for them, and re-layouts: 0.01 us -> 6.77 us
    convert_element_type x1 -> x4, other arithmetic: 7.53 us -> 3.34 us  [shards(): sent = piece.astype(BF16)]
  transfers between devices with their start and end apart: 3 -> 32, of which waited for: 3 -> 14; matrix products, arithmetic and copies ran while one was open for 0% -> 15% of each run, Pallas kernels for 0% -> 17%
where the time goes in v1:
time: 239 us
  waiting for transfers between devices  113 us (47%)
  Pallas kernels  52.6 us (22%)
  matrix products  31.2 us (13%)
  starting transfers between devices  26.9 us (11%)
  local copies, waits for them, and re-layouts  8.72 us (4%)
  other arithmetic  5.44 us (2%)
    ppermute x28, waiting for transfers between devices, swap(): return lax.ppermute(x, 'col', [(i, i ^ 1 << bit) for i in range(n)])  83.1 us
    pallas_call x4, Pallas kernels, back(): pl.pallas_call(functools.partial(back_body, n), grid=(m // t,), out_shape...  35.1 us
    dot_general x12, matrix products, project(): lax.dot_general(proj, grad, (((1,), (1,)), ((), ())), preferred_element_t...  31.2 us
    ppermute x4, waiting for transfers between devices, shift(): return lax.ppermute(x, 'row', [(i, (i + by) % n) for i in range(n)])  29.9 us
    ppermute x28, starting transfers between devices, swap(): return lax.ppermute(x, 'col', [(i, i ^ 1 << bit) for i in range(n)])  18.6 us
    pallas_call x4, Pallas kernels, adam(): pl.pallas_call(functools.partial(adam_body, n), grid=(m // t,), out_shape...  13.6 us
    ppermute x4, starting transfers between devices, shift(): return lax.ppermute(x, 'row', [(i, (i + by) % n) for i in range(n)])  8.32 us
    unnamed x55, local copies, waits for them, and re-layouts  6.77 us
  transfers between devices with their start and end apart: 32, of which 14 were waited for; matrix products, arithmetic and copies ran while one was open for 15% of the time, Pallas kernels for 17%

profile of v1, /device:TPU:0, one launch (start us, length us, event | category | flops | bytes accessed | tf_op | source)
XLA Modules:
  0.0 238.9 jit_solution(6595148602429777561)
XLA Ops:
  1.9 3.1 %collective-permute-start = (bf16[256,1024]{1,0:T(8,128)(2,1)S(1)}, bf16[256,1024]{1,0:T(8,128)(2,1)S(1)}, u32[]{:S(2)}, u32[]{:S(2)}) collective-permute-start(bf16[256,1024]{1,0:T(8,128)(2,1)S(1)} %bitcast.5), channel_id=1, source_target_pairs={{0,8},{8,16},{16,24},{24,0},{1,9},{9,17},{17,25},{25,1},{2,10},{10... | collective-permute-start | bytes 1572872 | tf_op jit(solution)/shard_map/ppermute | solution.py:21
  5.0 2.1 collective-permute-start.2
  7.1 12.8 %collective-permute-done.refs_2_ = bf16[256,1024]{1,0:T(8,128)(2,1)S(1)} collective-permute-done((bf16[256,1024]{1,0:T(8,128)(2,1)S(1)}, bf16[256,1024]{1,0:T(8,128)(2,1)S(1)}, u32[]{:S(2)}, u32[]{:S(2)}) %collective-permute-start) | collective-permute-done | bytes 524320 | tf_op jit(solution)/shard_map/ppermute | solution.py:21
  19.9 9.9 %collective-permute-done.2.refs_4_ = bf16[256,1024]{1,0:T(8,128)(2,1)S(1)} collective-permute-done((bf16[256,1024]{1,0:T(8,128)(2,1)S(1)}, bf16[256,1024]{1,0:T(8,128)(2,1)S(1)}, u32[]{:S(2)}, u32[]{:S(2)}) %collective-permute-start.2) | collective-permute-done | bytes 524320 | tf_op jit(solution)/shard_map/ppermute | solution.py:21
  29.9 3.1 %collective-permute-start.3 = (bf16[128,1024]{1,0:T(8,128)(2,1)S(1)}, bf16[128,1024]{1,0:T(8,128)(2,1)S(1)}, u32[]{:S(2)}, u32[]{:S(2)}) collective-permute-start(bf16[128,1024]{1,0:T(8,128)(2,1)S(1)} %slice.137), channel_id=1, source_target_pairs={{0,24},{8,0},{16,8},{24,16},{1,25},{9,1},{17,9},{25,17},{2,26},{10... | collective-permute-start | bytes 786440 | tf_op jit(solution)/shard_map/ppermute | solution.py:21
  34.2 4.2 %collective-permute-done.1 = bf16[128,1024]{1,0:T(8,128)(2,1)S(1)} collective-permute-done((bf16[128,1024]{1,0:T(8,128)(2,1)S(1)}, bf16[128,1024]{1,0:T(8,128)(2,1)S(1)}, u32[]{:S(2)}, u32[]{:S(2)}) %collective-permute-start.1) | collective-permute-done | bytes 262176 | tf_op jit(solution)/shard_map/ppermute | solution.py:21
  38.4 3.0 %collective-permute-done.3 = bf16[128,1024]{1,0:T(8,128)(2,1)S(1)} collective-permute-done((bf16[128,1024]{1,0:T(8,128)(2,1)S(1)}, bf16[128,1024]{1,0:T(8,128)(2,1)S(1)}, u32[]{:S(2)}, u32[]{:S(2)}) %collective-permute-start.3) | collective-permute-done | bytes 262176 | tf_op jit(solution)/shard_map/ppermute | solution.py:21
  42.3 4.0 %pick.1 = (bf16[1024,1024]{1,0:T(8,128)(2,1)}, bf16[1024,1024]{1,0:T(8,128)(2,1)}) custom-call(s32[2,8]{1,0:T(2,128)} %pad_add_fusion.refs_0_, bf16[256,1024]{1,0:T(8,128)(2,1)} %bitcast.7, bf16[256,1024]{1,0:T(8,128)(2,1)} %copy-done.16, bf16[256,1024]{1,0:T(8,128)(2,1)} %pad_maximum_fusion.refs_3_, bf16[256,1024]{1,0:T(8,128)(2,1)} %copy-done.17), custom_call_target="tpu_custom_call" | custom-call | tf_op jit(solution)/shard_map/pick/pallas_call | solution.py:57
  46.3 4.6 %convolution_convert_fusion.3 = bf16[512,1792]{1,0:T(8,128)(2,1)S(1)} fusion(bf16[7168,1024]{1,0:T(8,128)(2,1)} %param.6, bf16[1024,1024]{1,0:T(8,128)(2,1)} %get-tuple-element.22.refs_4_), kind=kOutput, calls=%fused_computation.3 | convolution fusion | flops 1879965696 | bytes 6553600 | tf_op jit(solution)/shard_map/dot_general | solution.py:151
  51.0 4.9 %convolution_convert_fusion.2 = bf16[512,1792]{1,0:T(8,128)(2,1)S(1)} fusion(bf16[7168,1024]{1,0:T(8,128)(2,1)} %param.6, bf16[1024,1024]{1,0:T(8,128)(2,1)S(1)} %copy-done), kind=kOutput, calls=%fused_computation.2 | convolution fusion | flops 1879965696 | bytes 6553600 | tf_op jit(solution)/shard_map/dot_general | solution.py:151
  64.3 3.4 %convolution_convert_fusion = bf16[512,1792]{1,0:T(8,128)(2,1)} fusion(bf16[7168,1024]{1,0:T(8,128)(2,1)S(1)} %copy-done.24, bf16[1024,1024]{1,0:T(8,128)(2,1)S(1)} %copy-done.1), kind=kOutput, calls=%fused_computation | convolution fusion | flops 1879965696 | bytes 6553600 | tf_op jit(solution)/shard_map/dot_general | solution.py:151
  67.7 3.3 %convolution_convert_fusion.1 = bf16[512,1792]{1,0:T(8,128)(2,1)} fusion(bf16[7168,1024]{1,0:T(8,128)(2,1)S(1)} %copy-done.24, bf16[1024,1024]{1,0:T(8,128)(2,1)S(1)} %copy-done), kind=kOutput, calls=%fused_computation.1 | convolution fusion | flops 1879965696 | bytes 6553600 | tf_op jit(solution)/shard_map/dot_general | solution.py:151
  71.5 10.8 %collective-permute-done.14.refs_2_ = bf16[256,1792]{1,0:T(8,128)(2,1)S(1)} collective-permute-done((bf16[256,1792]{1,0:T(8,128)(2,1)S(1)}, bf16[256,1792]{1,0:T(8,128)(2,1)S(1)}, u32[]{:S(2)}, u32[]{:S(2)}) %collective-permute-start.14) | collective-permute-done | bytes 917536 | tf_op jit(solution)/shard_map/ppermute | solution.py:17
  86.1 2.1 fusion.35.refs_0_
  89.4 5.4 %collective-permute-done.15.refs_3_ = bf16[128,1792]{1,0:T(8,128)(2,1)} collective-permute-done((bf16[128,1792]{1,0:T(8,128)(2,1)S(1)}, bf16[128,1792]{1,0:T(8,128)(2,1)}, u32[]{:S(2)}, u32[]{:S(2)}) %collective-permute-start.15) | collective-permute-done | bytes 458784 | tf_op jit(solution)/shard_map/ppermute | solution.py:17
  94.7 3.4 %adam.4 = (bf16[128,1792]{1,0:T(8,128)(2,1)}, f32[128,7168]{1,0:T(8,128)}, f32[128,7168]{1,0:T(8,128)}) custom-call(bf16[256,1792]{1,0:T(8,128)(2,1)} %copy-done.12, bf16[512,1792]{1,0:T(8,128)(2,1)} %copy-done.3, bf16[256,1792]{1,0:T(8,128)(2,1)} %copy-done.15, bf16[128,1792]{1,0:T(8,128)(2,1)} %collective-permute-done.15.refs_3_, f32[128,7168]{1,0:T(8,128)} %refs_4_.7, ...), custom_call_target="tpu_custom_call" | custom-call | flops 4587520 | bytes 5505024 | tf_op jit(solution)/shard_map/adam/pallas_call | solution.py:104
  99.7 3.4 %adam.5 = (bf16[128,1792]{1,0:T(8,128)(2,1)}, f32[128,7168]{1,0:T(8,128)}, f32[128,7168]{1,0:T(8,128)}) custom-call(bf16[256,1792]{1,0:T(8,128)(2,1)} %copy-done.11, bf16[512,1792]{1,0:T(8,128)(2,1)} %copy-done.2, bf16[256,1792]{1,0:T(8,128)(2,1)} %copy-done.13, ...), custom_call_target="tpu_custom_call", output_to_operand_aliasing={{1}: (6, {}), {2}: (7, {})} | custom-call | flops 4587520 | bytes 5505024 | tf_op jit(solution)/shard_map/adam/pallas_call | solution.py:104
  104.2 3.6 %add_convert_fusion = bf16[256,1792]{1,0:T(8,128)(2,1)S(1)} fusion(bf16[512,1792]{1,0:T(8,128)(2,1)} %collective-permute-done.9.refs_1_, bf16[7168,1024]{1,0:T(8,128)(2,1)} %param.6, bf16[1024,1024]{1,0:T(8,128)(2,1)} %get-tuple-element.22.refs_4_), kind=kOutput, calls=%fused_computation.32 | convolution fusion | flops 940900352 | bytes 6029312 | tf_op jit(solution)/shard_map/dot_general | solution.py:151
  108.9 3.4 %add_convert_fusion.1 = bf16[256,1792]{1,0:T(8,128)(2,1)S(1)} fusion(bf16[512,1792]{1,0:T(8,128)(2,1)} %collective-permute-done.6.refs_1_, bf16[7168,1024]{1,0:T(8,128)(2,1)} %param.6, bf16[1024,1024]{1,0:T(8,128)(2,1)S(1)} %copy-done), kind=kOutput, calls=%fused_computation.33 | convolution fusion | flops 940900352 | bytes 6029312 | tf_op jit(solution)/shard_map/dot_general | solution.py:151
  112.9 1.8 constant_dynamic-update-slice_fusion.7
  116.6 19.8 %collective-permute-done.10.refs_2_ = bf16[256,1792]{1,0:T(8,128)(2,1)S(1)} collective-permute-done((bf16[256,1792]{1,0:T(8,128)(2,1)S(1)}, bf16[256,1792]{1,0:T(8,128)(2,1)S(1)}, u32[]{:S(2)}, u32[]{:S(2)}) %collective-permute-start.10) | collective-permute-done | bytes 917536 | tf_op jit(solution)/shard_map/ppermute | solution.py:17
  141.1 5.3 %collective-permute-done.11.refs_3_ = bf16[128,1792]{1,0:T(8,128)(2,1)S(1)} collective-permute-done((bf16[128,1792]{1,0:T(8,128)(2,1)S(1)}, bf16[128,1792]{1,0:T(8,128)(2,1)S(1)}, u32[]{:S(2)}, u32[]{:S(2)}) %collective-permute-start.11) | collective-permute-done | bytes 458784 | tf_op jit(solution)/shard_map/ppermute | solution.py:17
  147.2 3.4 %adam.6 = (bf16[128,1792]{1,0:T(8,128)(2,1)}, f32[128,7168]{1,0:T(8,128)}, f32[128,7168]{1,0:T(8,128)}) custom-call(bf16[256,1792]{1,0:T(8,128)(2,1)} %fusion.35.refs_0_, bf16[512,1792]{1,0:T(8,128)(2,1)} %collective-permute-done.9.refs_1_, bf16[256,1792]{1,0:T(8,128)(2,1)} %copy-done.14, ...), custom_call_target="tpu_custom_call", output_to_operand_aliasing={{1}: (6, {}), {2}: (7, {})} | custom-call | flops 4587520 | bytes 5505024 | tf_op jit(solution)/shard_map/adam/pallas_call | solution.py:104
  154.0 2.2 collective-permute-done.29.refs_2_
  156.2 7.2 %collective-permute-done.8.refs_3_ = bf16[128,1792]{1,0:T(8,128)(2,1)S(1)} collective-permute-done((bf16[128,1792]{1,0:T(8,128)(2,1)S(1)}, bf16[128,1792]{1,0:T(8,128)(2,1)S(1)}, u32[]{:S(2)}, u32[]{:S(2)}) %collective-permute-start.8) | collective-permute-done | bytes 458784 | tf_op jit(solution)/shard_map/ppermute | solution.py:17
  164.2 3.4 %adam.7 = (bf16[128,1792]{1,0:T(8,128)(2,1)}, f32[128,7168]{1,0:T(8,128)}, f32[128,7168]{1,0:T(8,128)}) custom-call(bf16[256,1792]{1,0:T(8,128)(2,1)} %copy-done.8, bf16[512,1792]{1,0:T(8,128)(2,1)} %collective-permute-done.6.refs_1_, bf16[256,1792]{1,0:T(8,128)(2,1)} %copy-done.10, ...), custom_call_target="tpu_custom_call", output_to_operand_aliasing={{1}: (6, {}), {2}: (7, {})} | custom-call | flops 4587520 | bytes 5505024 | tf_op jit(solution)/shard_map/adam/pallas_call | solution.py:104
  168.4 11.7 %collective-permute-done.16 = bf16[128,1792]{1,0:T(8,128)(2,1)S(1)} collective-permute-done((bf16[128,1792]{1,0:T(8,128)(2,1)}, bf16[128,1792]{1,0:T(8,128)(2,1)S(1)}, u32[]{:S(2)}, u32[]{:S(2)}) %collective-permute-start.16) | collective-permute-done | bytes 458784 | tf_op jit(solution)/shard_map/ppermute | solution.py:17
  182.9 18.5 %collective-permute-done.21.refs_2_ = bf16[256,1792]{1,0:T(8,128)(2,1)} collective-permute-done((bf16[256,1792]{1,0:T(8,128)(2,1)S(1)}, bf16[256,1792]{1,0:T(8,128)(2,1)}, u32[]{:S(2)}, u32[]{:S(2)}) %collective-permute-start.21) | collective-permute-done | bytes 917536 | tf_op jit(solution)/shard_map/ppermute | solution.py:17
  202.8 8.8 %back.4.refs_5_ = f32[7168,1024]{1,0:T(8,128)} custom-call(bf16[256,1792]{1,0:T(8,128)(2,1)} %collective-permute-done.30.refs_0_, bf16[256,1792]{1,0:T(8,128)(2,1)} %collective-permute-done.31.refs_1_, bf16[256,1792]{1,0:T(8,128)(2,1)} %collective-permute-done.29.refs_2_, bf16[256,1792]{1,0:T(8,128)(2,1)} %constant_dynamic-update-slice_fusion.6.refs_3_, ...), custom_call_target="tpu_custom_call" | custom-call | flops 3758096384 | bytes 11010048 | tf_op jit(solution)/shard_map/back/pallas_call | solution.py:135
  211.6 8.8 %back.5.refs_5_ = f32[7168,1024]{1,0:T(8,128)} custom-call(bf16[256,1792]{1,0:T(8,128)(2,1)} %collective-permute-done.26.refs_0_, bf16[256,1792]{1,0:T(8,128)(2,1)} %collective-permute-done.27.refs_1_, bf16[256,1792]{1,0:T(8,128)(2,1)} %collective-permute-done.25.refs_2_, bf16[256,1792]{1,0:T(8,128)(2,1)} %copy-done.5, ...), custom_call_target="tpu_custom_call", output_to_operand_aliasing={{}: (5, {})} | custom-call | flops 3758096384 | bytes 11010048 | tf_op jit(solution)/shard_map/back/pallas_call | solution.py:135
  221.4 8.8 %back.6.refs_5_ = f32[7168,1024]{1,0:T(8,128)} custom-call(bf16[256,1792]{1,0:T(8,128)(2,1)} %collective-permute-done.22.refs_0_, bf16[256,1792]{1,0:T(8,128)(2,1)} %copy-done.18, bf16[256,1792]{1,0:T(8,128)(2,1)} %collective-permute-done.21.refs_2_, bf16[256,1792]{1,0:T(8,128)(2,1)} %copy-done.6, ...), custom_call_target="tpu_custom_call", output_to_operand_aliasing={{}: (5, {})} | custom-call | flops 3758096384 | bytes 11010048 | tf_op jit(solution)/shard_map/back/pallas_call | solution.py:135
  230.1 8.8 %back.7 = f32[7168,1024]{1,0:T(8,128)} custom-call(bf16[256,1792]{1,0:T(8,128)(2,1)} %collective-permute-done.18.refs_0_, bf16[256,1792]{1,0:T(8,128)(2,1)} %collective-permute-done.19.refs_1_, bf16[256,1792]{1,0:T(8,128)(2,1)} %collective-permute-done.17.refs_2_, bf16[256,1792]{1,0:T(8,128)(2,1)} %copy-done.7, ...), custom_call_target="tpu_custom_call", output_to_operand_aliasing={{}: (5, {})} | custom-call | flops 3758096384 | bytes 11010048 | tf_op jit(solution)/shard_map/back/pallas_call | solution.py:135
  (121 shorter events, 38.9 us)
Async XLA Ops:
  1.9 17.9 %collective-permute-start = (bf16[256,1024]{1,0:T(8,128)(2,1)S(1)}, bf16[256,1024]{1,0:T(8,128)(2,1)S(1)}, u32[]{:S(2)}, u32[]{:S(2)}) collective-permute-start(bf16[256,1024]{1,0:T(8,128)(2,1)S(1)} %bitcast.5), channel_id=1, source_target_pairs={{0,8},{8,16},{16,24},{24,0},{1,9},{9,17},{17,25},{25,1},{2,10},{10... | collective-permute-start | bytes 1572872 | tf_op jit(solution)/shard_map/ppermute | solution.py:21
  5.0 24.9 %collective-permute-start.2 = (bf16[256,1024]{1,0:T(8,128)(2,1)S(1)}, bf16[256,1024]{1,0:T(8,128)(2,1)S(1)}, u32[]{:S(2)}, u32[]{:S(2)}) collective-permute-start(bf16[256,1024]{1,0:T(8,128)(2,1)S(1)} %bitcast.6), channel_id=1, source_target_pairs={{0,24},{8,0},{16,8},{24,16},{1,25},{9,1},{17,9},{25,17},{2,26},{10... | collective-permute-start | bytes 1572872 | tf_op jit(solution)/shard_map/ppermute | solution.py:21
  19.9 18.6 %collective-permute-start.1 = (bf16[128,1024]{1,0:T(8,128)(2,1)S(1)}, bf16[128,1024]{1,0:T(8,128)(2,1)S(1)}, u32[]{:S(2)}, u32[]{:S(2)}) collective-permute-start(bf16[128,1024]{1,0:T(8,128)(2,1)S(1)} %slice.136), channel_id=1, source_target_pairs={{0,8},{8,16},{16,24},{24,0},{1,9},{9,17},{17,25},{25,1},{2,10},{10... | collective-permute-start | bytes 786440 | tf_op jit(solution)/shard_map/ppermute | solution.py:21
  29.9 11.6 %collective-permute-start.3 = (bf16[128,1024]{1,0:T(8,128)(2,1)S(1)}, bf16[128,1024]{1,0:T(8,128)(2,1)S(1)}, u32[]{:S(2)}, u32[]{:S(2)}) collective-permute-start(bf16[128,1024]{1,0:T(8,128)(2,1)S(1)} %slice.137), channel_id=1, source_target_pairs={{0,24},{8,0},{16,8},{24,16},{1,25},{9,1},{17,9},{25,17},{2,26},{10... | collective-permute-start | bytes 786440 | tf_op jit(solution)/shard_map/ppermute | solution.py:21
  50.9 8.0 %collective-permute-start.4 = (bf16[512,1792]{1,0:T(8,128)(2,1)S(1)}, bf16[512,1792]{1,0:T(8,128)(2,1)S(1)}, u32[]{:S(2)}, u32[]{:S(2)}) collective-permute-start(bf16[512,1792]{1,0:T(8,128)(2,1)S(1)} %convolution_convert_fusion.3), channel_id=1, source_target_pairs={{0,1},{1,0},{2,3},{3,2},{4,5},{5,4},{6,7},{7,6},{8,9},{9,8},{10,11... | collective-permute-start | bytes 5505032 | tf_op jit(solution)/shard_map/ppermute | solution.py:17
  55.9 5.7 %collective-permute-start.5 = (bf16[512,1792]{1,0:T(8,128)(2,1)S(1)}, bf16[512,1792]{1,0:T(8,128)(2,1)S(1)}, u32[]{:S(2)}, u32[]{:S(2)}) collective-permute-start(bf16[512,1792]{1,0:T(8,128)(2,1)S(1)} %convolution_convert_fusion.2), channel_id=1, source_target_pairs={{0,1},{1,0},{2,3},{3,2},{4,5},{5,4},{6,7},{7,6},{8,9},{9,8},{10,11... | collective-permute-start | bytes 5505032 | tf_op jit(solution)/shard_map/ppermute | solution.py:17
  60.0 22.3 %collective-permute-start.14 = (bf16[256,1792]{1,0:T(8,128)(2,1)S(1)}, bf16[256,1792]{1,0:T(8,128)(2,1)S(1)}, u32[]{:S(2)}, u32[]{:S(2)}) collective-permute-start(bf16[256,1792]{1,0:T(8,128)(2,1)S(1)} %fusion.41), channel_id=1, source_target_pairs={{0,2},{1,3},{2,0},{3,1},{4,6},{5,7},{6,4},{7,5},{8,10},{9,11},{10,... | collective-permute-start | bytes 2752520 | tf_op jit(solution)/shard_map/ppermute | solution.py:17
  62.7 22.5 %collective-permute-start.12 = (bf16[256,1792]{1,0:T(8,128)(2,1)S(1)}, bf16[256,1792]{1,0:T(8,128)(2,1)S(1)}, u32[]{:S(2)}, u32[]{:S(2)}) collective-permute-start(bf16[256,1792]{1,0:T(8,128)(2,1)S(1)} %fusion.38), channel_id=1, source_target_pairs={{0,4},{1,5},{2,6},{3,7},{4,0},{5,1},{6,2},{7,3},{8,12},{9,13},{10,... | collective-permute-start | bytes 2752520 | tf_op jit(solution)/shard_map/ppermute | solution.py:17
  67.7 36.5 %collective-permute-start.9 = (bf16[512,1792]{1,0:T(8,128)(2,1)}, bf16[512,1792]{1,0:T(8,128)(2,1)}, u32[]{:S(2)}, u32[]{:S(2)}) collective-permute-start(bf16[512,1792]{1,0:T(8,128)(2,1)} %convolution_convert_fusion), channel_id=1, source_target_pairs={{0,1},{1,0},{2,3},{3,2},{4,5},{5,4},{6,7},{7,6},{8,9},{9,8},{10,11... | collective-permute-start | bytes 5505032 | tf_op jit(solution)/shard_map/ppermute | solution.py:17
  71.0 37.8 %collective-permute-start.6 = (bf16[512,1792]{1,0:T(8,128)(2,1)}, bf16[512,1792]{1,0:T(8,128)(2,1)}, u32[]{:S(2)}, u32[]{:S(2)}) collective-permute-start(bf16[512,1792]{1,0:T(8,128)(2,1)} %convolution_convert_fusion.1), channel_id=1, source_target_pairs={{0,1},{1,0},{2,3},{3,2},{4,5},{5,4},{6,7},{7,6},{8,9},{9,8},{10,11... | collective-permute-start | bytes 5505032 | tf_op jit(solution)/shard_map/ppermute | solution.py:17
  82.5 12.2 %collective-permute-start.15 = (bf16[128,1792]{1,0:T(8,128)(2,1)S(1)}, bf16[128,1792]{1,0:T(8,128)(2,1)}, u32[]{:S(2)}, u32[]{:S(2)}) collective-permute-start(bf16[128,1792]{1,0:T(8,128)(2,1)S(1)} %add_convert_fusion.2), channel_id=1, source_target_pairs={{0,4},{1,5},{2,6},{3,7},{4,0},{5,1},{6,2},{7,3},{8,12},{9,13},{10,... | collective-permute-start | bytes 1376264 | tf_op jit(solution)/shard_map/ppermute | solution.py:17
  85.4 14.3 %collective-permute-start.13 = (bf16[128,1792]{1,0:T(8,128)(2,1)S(1)}, bf16[128,1792]{1,0:T(8,128)(2,1)}, u32[]{:S(2)}, u32[]{:S(2)}) collective-permute-start(bf16[128,1792]{1,0:T(8,128)(2,1)S(1)} %add_convert_fusion.3), channel_id=1, source_target_pairs={{0,2},{1,3},{2,0},{3,1},{4,6},{5,7},{6,4},{7,5},{8,10},{9,11},{10,... | collective-permute-start | bytes 1376264 | tf_op jit(solution)/shard_map/ppermute | solution.py:17
  98.1 14.8 %collective-permute-start.28 = (bf16[128,1792]{1,0:T(8,128)(2,1)}, bf16[128,1792]{1,0:T(8,128)(2,1)}, u32[]{:S(2)}, u32[]{:S(2)}) collective-permute-start(bf16[128,1792]{1,0:T(8,128)(2,1)} %get-tuple-element.32), channel_id=1, source_target_pairs={{0,4},{1,5},{2,6},{3,7},{4,0},{5,1},{6,2},{7,3},{8,12},{9,13},{10,... | collective-permute-start | bytes 1376264 | tf_op jit(solution)/shard_map/ppermute | solution.py:17
  103.1 48.2 %collective-permute-start.24 = (bf16[128,1792]{1,0:T(8,128)(2,1)}, bf16[128,1792]{1,0:T(8,128)(2,1)}, u32[]{:S(2)}, u32[]{:S(2)}) collective-permute-start(bf16[128,1792]{1,0:T(8,128)(2,1)} %get-tuple-element.31), channel_id=1, source_target_pairs={{0,2},{1,3},{2,0},{3,1},{4,6},{5,7},{6,4},{7,5},{8,10},{9,11},{10,... | collective-permute-start | bytes 1376264 | tf_op jit(solution)/shard_map/ppermute | solution.py:17
  107.8 28.6 %collective-permute-start.10 = (bf16[256,1792]{1,0:T(8,128)(2,1)S(1)}, bf16[256,1792]{1,0:T(8,128)(2,1)S(1)}, u32[]{:S(2)}, u32[]{:S(2)}) collective-permute-start(bf16[256,1792]{1,0:T(8,128)(2,1)S(1)} %add_convert_fusion), channel_id=1, source_target_pairs={{0,2},{1,3},{2,0},{3,1},{4,6},{5,7},{6,4},{7,5},{8,10},{9,11},{10,... | collective-permute-start | bytes 2752520 | tf_op jit(solution)/shard_map/ppermute | solution.py:17
  112.3 26.2 %collective-permute-start.7 = (bf16[256,1792]{1,0:T(8,128)(2,1)S(1)}, bf16[256,1792]{1,0:T(8,128)(2,1)S(1)}, u32[]{:S(2)}, u32[]{:S(2)}) collective-permute-start(bf16[256,1792]{1,0:T(8,128)(2,1)S(1)} %add_convert_fusion.1), channel_id=1, source_target_pairs={{0,4},{1,5},{2,6},{3,7},{4,0},{5,1},{6,2},{7,3},{8,12},{9,13},{10,... | collective-permute-start | bytes 2752520 | tf_op jit(solution)/shard_map/ppermute | solution.py:17
  115.5 40.6 %collective-permute-start.29 = (bf16[256,1792]{1,0:T(8,128)(2,1)}, bf16[256,1792]{1,0:T(8,128)(2,1)}, u32[]{:S(2)}, u32[]{:S(2)}) collective-permute-start(bf16[256,1792]{1,0:T(8,128)(2,1)} %constant_dynamic-update-slice_fusion.6.refs_3_), channel_id=1, source_target_pairs={{0,2},{1,3},{2,0},{3,1},{4,6},{5,7},{6,4},{7,5},{8,10},{9,11},{10,... | collective-permute-start | bytes 2752520 | tf_op jit(solution)/shard_map/ppermute | solution.py:17
  116.6 65.2 %collective-permute-start.31 = (bf16[256,1792]{1,0:T(8,128)(2,1)}, bf16[256,1792]{1,0:T(8,128)(2,1)}, u32[]{:S(2)}, u32[]{:S(2)}) collective-permute-start(bf16[256,1792]{1,0:T(8,128)(2,1)} %constant_dynamic-update-slice_fusion.6.refs_3_), channel_id=1, source_target_pairs={{0,1},{1,0},{2,3},{3,2},{4,5},{5,4},{6,7},{7,6},{8,9},{9,8},{10,11... | collective-permute-start | bytes 2752520 | tf_op jit(solution)/shard_map/ppermute | solution.py:17
  137.9 8.5 %collective-permute-start.11 = (bf16[128,1792]{1,0:T(8,128)(2,1)S(1)}, bf16[128,1792]{1,0:T(8,128)(2,1)S(1)}, u32[]{:S(2)}, u32[]{:S(2)}) collective-permute-start(bf16[128,1792]{1,0:T(8,128)(2,1)S(1)} %add_convert_fusion.4), channel_id=1, source_target_pairs={{0,4},{1,5},{2,6},{3,7},{4,0},{5,1},{6,2},{7,3},{8,12},{9,13},{10,... | collective-permute-start | bytes 1376264 | tf_op jit(solution)/shard_map/ppermute | solution.py:17
  140.0 23.4 %collective-permute-start.8 = (bf16[128,1792]{1,0:T(8,128)(2,1)S(1)}, bf16[128,1792]{1,0:T(8,128)(2,1)S(1)}, u32[]{:S(2)}, u32[]{:S(2)}) collective-permute-start(bf16[128,1792]{1,0:T(8,128)(2,1)S(1)} %add_convert_fusion.5), channel_id=1, source_target_pairs={{0,2},{1,3},{2,0},{3,1},{4,6},{5,7},{6,4},{7,5},{8,10},{9,11},{10,... | collective-permute-start | bytes 1376264 | tf_op jit(solution)/shard_map/ppermute | solution.py:17
  150.7 16.9 %collective-permute-start.20 = (bf16[128,1792]{1,0:T(8,128)(2,1)}, bf16[128,1792]{1,0:T(8,128)(2,1)S(1)}, u32[]{:S(2)}, u32[]{:S(2)}) collective-permute-start(bf16[128,1792]{1,0:T(8,128)(2,1)} %get-tuple-element.30), channel_id=1, source_target_pairs={{0,4},{1,5},{2,6},{3,7},{4,0},{5,1},{6,2},{7,3},{8,12},{9,13},{10,... | collective-permute-start | bytes 1376264 | tf_op jit(solution)/shard_map/ppermute | solution.py:17
  152.4 30.0 %collective-permute-start.25 = (bf16[256,1792]{1,0:T(8,128)(2,1)S(1)}, bf16[256,1792]{1,0:T(8,128)(2,1)}, u32[]{:S(2)}, u32[]{:S(2)}) collective-permute-start(bf16[256,1792]{1,0:T(8,128)(2,1)S(1)} %constant_dynamic-update-slice_fusion.4.refs_3_), channel_id=1, source_target_pairs={{0,4},{1,5},{2,6},{3,7},{4,0},{5,1},{6,2},{7,3},{8,12},{9,13},{10,... | collective-permute-start | bytes 2752520 | tf_op jit(solution)/shard_map/ppermute | solution.py:17
  156.2 26.2 %collective-permute-start.27 = (bf16[256,1792]{1,0:T(8,128)(2,1)S(1)}, bf16[256,1792]{1,0:T(8,128)(2,1)}, u32[]{:S(2)}, u32[]{:S(2)}) collective-permute-start(bf16[256,1792]{1,0:T(8,128)(2,1)S(1)} %constant_dynamic-update-slice_fusion.4.refs_3_), channel_id=1, source_target_pairs={{0,1},{1,0},{2,3},{3,2},{4,5},{5,4},{6,7},{7,6},{8,9},{9,8},{10,11... | collective-permute-start | bytes 2752520 | tf_op jit(solution)/shard_map/ppermute | solution.py:17
  163.4 37.9 %collective-permute-start.30 = (bf16[256,1792]{1,0:T(8,128)(2,1)}, bf16[256,1792]{1,0:T(8,128)(2,1)}, u32[]{:S(2)}, u32[]{:S(2)}) collective-permute-start(bf16[256,1792]{1,0:T(8,128)(2,1)} %collective-permute-done.29.refs_2_), channel_id=1, source_target_pairs={{0,1},{1,0},{2,3},{3,2},{4,5},{5,4},{6,7},{7,6},{8,9},{9,8},{10,11... | collective-permute-start | bytes 2752520 | tf_op jit(solution)/shard_map/ppermute | solution.py:17
  167.6 12.5 %collective-permute-start.16 = (bf16[128,1792]{1,0:T(8,128)(2,1)}, bf16[128,1792]{1,0:T(8,128)(2,1)S(1)}, u32[]{:S(2)}, u32[]{:S(2)}) collective-permute-start(bf16[128,1792]{1,0:T(8,128)(2,1)} %get-tuple-element.29), channel_id=1, source_target_pairs={{0,2},{1,3},{2,0},{3,1},{4,6},{5,7},{6,4},{7,5},{8,10},{9,11},{10,... | collective-permute-start | bytes 1376264 | tf_op jit(solution)/shard_map/ppermute | solution.py:17
  180.1 21.3 %collective-permute-start.21 = (bf16[256,1792]{1,0:T(8,128)(2,1)S(1)}, bf16[256,1792]{1,0:T(8,128)(2,1)}, u32[]{:S(2)}, u32[]{:S(2)}) collective-permute-start(bf16[256,1792]{1,0:T(8,128)(2,1)S(1)} %constant_dynamic-update-slice_fusion.2.refs_3_), channel_id=1, source_target_pairs={{0,2},{1,3},{2,0},{3,1},{4,6},{5,7},{6,4},{7,5},{8,10},{9,11},{10,... | collective-permute-start | bytes 2752520 | tf_op jit(solution)/shard_map/ppermute | solution.py:17
  181.8 21.0 %collective-permute-start.17 = (bf16[256,1792]{1,0:T(8,128)(2,1)S(1)}, bf16[256,1792]{1,0:T(8,128)(2,1)}, u32[]{:S(2)}, u32[]{:S(2)}) collective-permute-start(bf16[256,1792]{1,0:T(8,128)(2,1)S(1)} %constant_dynamic-update-slice_fusion.refs_3_), channel_id=1, source_target_pairs={{0,4},{1,5},{2,6},{3,7},{4,0},{5,1},{6,2},{7,3},{8,12},{9,13},{10,... | collective-permute-start | bytes 2752520 | tf_op jit(solution)/shard_map/ppermute | solution.py:17
  182.4 29.2 %collective-permute-start.26 = (bf16[256,1792]{1,0:T(8,128)(2,1)}, bf16[256,1792]{1,0:T(8,128)(2,1)}, u32[]{:S(2)}, u32[]{:S(2)}) collective-permute-start(bf16[256,1792]{1,0:T(8,128)(2,1)} %collective-permute-done.25.refs_2_), channel_id=1, source_target_pairs={{0,1},{1,0},{2,3},{3,2},{4,5},{5,4},{6,7},{7,6},{8,9},{9,8},{10,11... | collective-permute-start | bytes 2752520 | tf_op jit(solution)/shard_map/ppermute | solution.py:17
  182.4 38.0 %collective-permute-start.23 = (bf16[256,1792]{1,0:T(8,128)(2,1)S(1)}, bf16[256,1792]{1,0:T(8,128)(2,1)S(1)}, u32[]{:S(2)}, u32[]{:S(2)}) collective-permute-start(bf16[256,1792]{1,0:T(8,128)(2,1)S(1)} %constant_dynamic-update-slice_fusion.2.refs_3_), channel_id=1, source_target_pairs={{0,1},{1,0},{2,3},{3,2},{4,5},{5,4},{6,7},{7,6},{8,9},{9,8},{10,11... | collective-permute-start | bytes 2752520 | tf_op jit(solution)/shard_map/ppermute | solution.py:17
  201.3 19.1 %collective-permute-start.22 = (bf16[256,1792]{1,0:T(8,128)(2,1)}, bf16[256,1792]{1,0:T(8,128)(2,1)}, u32[]{:S(2)}, u32[]{:S(2)}) collective-permute-start(bf16[256,1792]{1,0:T(8,128)(2,1)} %collective-permute-done.21.refs_2_), channel_id=1, source_target_pairs={{0,1},{1,0},{2,3},{3,2},{4,5},{5,4},{6,7},{7,6},{8,9},{9,8},{10,11... | collective-permute-start | bytes 2752520 | tf_op jit(solution)/shard_map/ppermute | solution.py:17
  201.3 28.8 %collective-permute-start.19 = (bf16[256,1792]{1,0:T(8,128)(2,1)S(1)}, bf16[256,1792]{1,0:T(8,128)(2,1)}, u32[]{:S(2)}, u32[]{:S(2)}) collective-permute-start(bf16[256,1792]{1,0:T(8,128)(2,1)S(1)} %constant_dynamic-update-slice_fusion.refs_3_), channel_id=1, source_target_pairs={{0,1},{1,0},{2,3},{3,2},{4,5},{5,4},{6,7},{7,6},{8,9},{9,8},{10,11... | collective-permute-start | bytes 2752520 | tf_op jit(solution)/shard_map/ppermute | solution.py:17
  202.8 27.3 %collective-permute-start.18 = (bf16[256,1792]{1,0:T(8,128)(2,1)}, bf16[256,1792]{1,0:T(8,128)(2,1)}, u32[]{:S(2)}, u32[]{:S(2)}) collective-permute-start(bf16[256,1792]{1,0:T(8,128)(2,1)} %collective-permute-done.17.refs_2_), channel_id=1, source_target_pairs={{0,1},{1,0},{2,3},{3,2},{4,5},{5,4},{6,7},{7,6},{8,9},{9,8},{10,11... | collective-permute-start | bytes 2752520 | tf_op jit(solution)/shard_map/ppermute | solution.py:17
  (25 other events, 403.3 us)

commit v2 on v1

--- a/solution.py
+++ b/solution.py
@@ -87,7 +87,7 @@
     s = 0.999 * second[...] + 0.001 * c * c
     corr_first = 1.0 - 0.9**10
     corr_second = 1.0 - 0.999**10
-    direction[...] = (f / corr_first / (jnp.sqrt(s / corr_second) + 1e-08)).astype(BF16)
+    direction[...] = (f / corr_first / (jnp.sqrt(s / corr_second) + 1e-08)).T.astype(BF16)
     first_next[...] = f
     second_next[...] = s
 
@@ -105,12 +105,12 @@
         functools.partial(adam_body, n),
         grid=(m // t,),
         out_shape=(
-            jax.ShapeDtypeStruct((rows, m), BF16),
+            jax.ShapeDtypeStruct((m, rows), BF16),
             jax.ShapeDtypeStruct((rows, cols), F32),
             jax.ShapeDtypeStruct((rows, cols), F32),
         ),
         in_specs=[last(x) for x in terms] + [whole, whole] + anywhere,
-        out_specs=(pl.BlockSpec((rows, t), lambda i: (0, i)), whole, whole),
+        out_specs=(pl.BlockSpec((t, rows), lambda i: (i, 0)), whole, whole),
         input_output_aliases={n + 2: 1, n + 3: 2} if moments else {},
         cost_estimate=pl.CostEstimate(
             flops=20 * rows * m, bytes_accessed=rows * m * 24, transcendentals=2 * rows * m
@@ -123,12 +123,12 @@
     pieces, proj, out = refs[:parts], refs[parts], refs[-1]
     t = out.shape[0]
     at = pl.ds(pl.multiple_of(pl.program_id(0) * t, t), t)
-    whole = jnp.concatenate([p[:, at] for p in pieces], axis=0)
-    out[...] = lax.dot_general(whole, proj[...], (((0,), (0,)), ((), ())), preferred_element_type=F32)
+    whole = jnp.concatenate([p[at] for p in pieces], axis=1)
+    out[...] = jnp.dot(whole, proj[...], preferred_element_type=F32)
 
 
 def back(offset, pieces, proj, total, update):
-    m = pieces[0].shape[1]
+    m = pieces[0].shape[0]
     ranks, width = proj.shape
     t = tile(m, offset)
     n = len(pieces)
@@ -205,7 +205,7 @@
         held = [direction]
         for k in reversed(range(levels)):
             if k:
-                whole = held[0] if len(held) == 1 else jnp.concatenate(held)
+                whole = held[0] if len(held) == 1 else jnp.concatenate(held, axis=1)
                 held = [swap(whole, bits[k], n_col), whole]
             else:
                 held = [swap(x, bits[k], n_col) for x in held] + held

time: 239 us -> 240 us (level)
  no operation moved by 1% of the time
where the time goes in v2:
time: 240 us; the launch traced here: 239 us
  waiting for transfers between devices  113 us (47%)
  Pallas kernels  53 us (22%)
  matrix products  31.2 us (13%)
  starting transfers between devices  26.9 us (11%)
  local copies, waits for them, and re-layouts  9.14 us (4%)
  other arithmetic  5.44 us (2%)
    ppermute x28, waiting for transfers between devices, swap(): return lax.ppermute(x, 'col', [(i, i ^ 1 << bit) for i in range(n)])  82.7 us
    pallas_call x4, Pallas kernels, back(): pl.pallas_call(functools.partial(back_body, n), grid=(m // t,), out_shape...  34.8 us
    dot_general x12, matrix products, project(): lax.dot_general(proj, grad, (((1,), (1,)), ((), ())), preferred_element_t...  31.2 us
    ppermute x4, waiting for transfers between devices, shift(): return lax.ppermute(x, 'row', [(i, (i + by) % n) for i in range(n)])  29.9 us
    ppermute x28, starting transfers between devices, swap(): return lax.ppermute(x, 'col', [(i, i ^ 1 << bit) for i in range(n)])  18.6 us
    pallas_call x4, Pallas kernels, adam(): pl.pallas_call(functools.partial(adam_body, n), grid=(m // t,), out_shape...  14.2 us
    ppermute x4, starting transfers between devices, shift(): return lax.ppermute(x, 'row', [(i, (i + by) % n) for i in range(n)])  8.32 us
    unnamed x55, local copies, waits for them, and re-layouts  6.92 us
  transfers between devices with their start and end apart: 32, of which 14 were waited for; matrix products, arithmetic and copies ran while one was open for 15% of the time, Pallas kernels for 17%

profile of v2, /device:TPU:0, one launch (start us, length us, event | category | flops | bytes accessed | tf_op | source)
XLA Modules:
  0.0 239.2 jit_solution(1389827889339591852)
XLA Ops:
  1.9 3.1 %collective-permute-start = (bf16[256,1024]{1,0:T(8,128)(2,1)S(1)}, bf16[256,1024]{1,0:T(8,128)(2,1)S(1)}, u32[]{:S(2)}, u32[]{:S(2)}) collective-permute-start(bf16[256,1024]{1,0:T(8,128)(2,1)S(1)} %bitcast.5), channel_id=1, source_target_pairs={{0,8},{8,16},{16,24},{24,0},{1,9},{9,17},{17,25},{25,1},{2,10},{10... | collective-permute-start | bytes 1572872 | tf_op jit(solution)/shard_map/ppermute | solution.py:21
  5.0 2.1 collective-permute-start.2
  7.1 12.8 %collective-permute-done.refs_2_ = bf16[256,1024]{1,0:T(8,128)(2,1)S(1)} collective-permute-done((bf16[256,1024]{1,0:T(8,128)(2,1)S(1)}, bf16[256,1024]{1,0:T(8,128)(2,1)S(1)}, u32[]{:S(2)}, u32[]{:S(2)}) %collective-permute-start) | collective-permute-done | bytes 524320 | tf_op jit(solution)/shard_map/ppermute | solution.py:21
  19.9 9.9 %collective-permute-done.2.refs_4_ = bf16[256,1024]{1,0:T(8,128)(2,1)S(1)} collective-permute-done((bf16[256,1024]{1,0:T(8,128)(2,1)S(1)}, bf16[256,1024]{1,0:T(8,128)(2,1)S(1)}, u32[]{:S(2)}, u32[]{:S(2)}) %collective-permute-start.2) | collective-permute-done | bytes 524320 | tf_op jit(solution)/shard_map/ppermute | solution.py:21
  29.9 3.1 %collective-permute-start.3 = (bf16[128,1024]{1,0:T(8,128)(2,1)S(1)}, bf16[128,1024]{1,0:T(8,128)(2,1)S(1)}, u32[]{:S(2)}, u32[]{:S(2)}) collective-permute-start(bf16[128,1024]{1,0:T(8,128)(2,1)S(1)} %slice.137), channel_id=1, source_target_pairs={{0,24},{8,0},{16,8},{24,16},{1,25},{9,1},{17,9},{25,17},{2,26},{10... | collective-permute-start | bytes 786440 | tf_op jit(solution)/shard_map/ppermute | solution.py:21
  34.2 4.2 %collective-permute-done.1 = bf16[128,1024]{1,0:T(8,128)(2,1)S(1)} collective-permute-done((bf16[128,1024]{1,0:T(8,128)(2,1)S(1)}, bf16[128,1024]{1,0:T(8,128)(2,1)S(1)}, u32[]{:S(2)}, u32[]{:S(2)}) %collective-permute-start.1) | collective-permute-done | bytes 262176 | tf_op jit(solution)/shard_map/ppermute | solution.py:21
  38.4 3.0 %collective-permute-done.3 = bf16[128,1024]{1,0:T(8,128)(2,1)S(1)} collective-permute-done((bf16[128,1024]{1,0:T(8,128)(2,1)S(1)}, bf16[128,1024]{1,0:T(8,128)(2,1)S(1)}, u32[]{:S(2)}, u32[]{:S(2)}) %collective-permute-start.3) | collective-permute-done | bytes 262176 | tf_op jit(solution)/shard_map/ppermute | solution.py:21
  42.3 4.0 %pick.1 = (bf16[1024,1024]{1,0:T(8,128)(2,1)}, bf16[1024,1024]{1,0:T(8,128)(2,1)}) custom-call(s32[2,8]{1,0:T(2,128)} %pad_add_fusion.refs_0_, bf16[256,1024]{1,0:T(8,128)(2,1)} %bitcast.7, bf16[256,1024]{1,0:T(8,128)(2,1)} %copy-done.16, bf16[256,1024]{1,0:T(8,128)(2,1)} %pad_maximum_fusion.refs_3_, bf16[256,1024]{1,0:T(8,128)(2,1)} %copy-done.17), custom_call_target="tpu_custom_call" | custom-call | tf_op jit(solution)/shard_map/pick/pallas_call | solution.py:57
  46.3 4.6 %convolution_convert_fusion.3 = bf16[512,1792]{1,0:T(8,128)(2,1)S(1)} fusion(bf16[7168,1024]{1,0:T(8,128)(2,1)} %param.6, bf16[1024,1024]{1,0:T(8,128)(2,1)} %get-tuple-element.22.refs_4_), kind=kOutput, calls=%fused_computation.3 | convolution fusion | flops 1879965696 | bytes 6553600 | tf_op jit(solution)/shard_map/dot_general | solution.py:151
  51.0 4.9 %convolution_convert_fusion.2 = bf16[512,1792]{1,0:T(8,128)(2,1)S(1)} fusion(bf16[7168,1024]{1,0:T(8,128)(2,1)} %param.6, bf16[1024,1024]{1,0:T(8,128)(2,1)S(1)} %copy-done), kind=kOutput, calls=%fused_computation.2 | convolution fusion | flops 1879965696 | bytes 6553600 | tf_op jit(solution)/shard_map/dot_general | solution.py:151
  64.3 3.4 %convolution_convert_fusion = bf16[512,1792]{1,0:T(8,128)(2,1)} fusion(bf16[7168,1024]{1,0:T(8,128)(2,1)S(1)} %copy-done.24, bf16[1024,1024]{1,0:T(8,128)(2,1)S(1)} %copy-done.1), kind=kOutput, calls=%fused_computation | convolution fusion | flops 1879965696 | bytes 6553600 | tf_op jit(solution)/shard_map/dot_general | solution.py:151
  67.7 3.3 %convolution_convert_fusion.1 = bf16[512,1792]{1,0:T(8,128)(2,1)} fusion(bf16[7168,1024]{1,0:T(8,128)(2,1)S(1)} %copy-done.24, bf16[1024,1024]{1,0:T(8,128)(2,1)S(1)} %copy-done), kind=kOutput, calls=%fused_computation.1 | convolution fusion | flops 1879965696 | bytes 6553600 | tf_op jit(solution)/shard_map/dot_general | solution.py:151
  71.5 10.8 %collective-permute-done.14.refs_2_ = bf16[256,1792]{1,0:T(8,128)(2,1)S(1)} collective-permute-done((bf16[256,1792]{1,0:T(8,128)(2,1)S(1)}, bf16[256,1792]{1,0:T(8,128)(2,1)S(1)}, u32[]{:S(2)}, u32[]{:S(2)}) %collective-permute-start.14) | collective-permute-done | bytes 917536 | tf_op jit(solution)/shard_map/ppermute | solution.py:17
  86.1 2.1 fusion.35.refs_0_
  89.4 5.4 %collective-permute-done.15.refs_3_ = bf16[128,1792]{1,0:T(8,128)(2,1)} collective-permute-done((bf16[128,1792]{1,0:T(8,128)(2,1)S(1)}, bf16[128,1792]{1,0:T(8,128)(2,1)}, u32[]{:S(2)}, u32[]{:S(2)}) %collective-permute-start.15) | collective-permute-done | bytes 458784 | tf_op jit(solution)/shard_map/ppermute | solution.py:17
  94.7 3.5 %adam.4 = (bf16[1792,128]{1,0:T(8,128)(2,1)}, f32[128,7168]{1,0:T(8,128)}, f32[128,7168]{1,0:T(8,128)}) custom-call(bf16[256,1792]{1,0:T(8,128)(2,1)} %copy-done.12, bf16[512,1792]{1,0:T(8,128)(2,1)} %copy-done.3, bf16[256,1792]{1,0:T(8,128)(2,1)} %copy-done.15, bf16[128,1792]{1,0:T(8,128)(2,1)} %collective-permute-done.15.refs_3_, f32[128,7168]{1,0:T(8,128)} %refs_4_.7, ...), custom_call_target="tpu_custom_call" | custom-call | flops 4587520 | bytes 5505024 | tf_op jit(solution)/shard_map/adam/pallas_call | solution.py:104
  99.8 3.5 %adam.5 = (bf16[1792,128]{1,0:T(8,128)(2,1)}, f32[128,7168]{1,0:T(8,128)}, f32[128,7168]{1,0:T(8,128)}) custom-call(bf16[256,1792]{1,0:T(8,128)(2,1)} %copy-done.11, bf16[512,1792]{1,0:T(8,128)(2,1)} %copy-done.2, bf16[256,1792]{1,0:T(8,128)(2,1)} %copy-done.13, ...), custom_call_target="tpu_custom_call", output_to_operand_aliasing={{1}: (6, {}), {2}: (7, {})} | custom-call | flops 4587520 | bytes 5505024 | tf_op jit(solution)/shard_map/adam/pallas_call | solution.py:104
  104.5 3.6 %add_convert_fusion = bf16[256,1792]{1,0:T(8,128)(2,1)S(1)} fusion(bf16[512,1792]{1,0:T(8,128)(2,1)} %collective-permute-done.9.refs_1_, bf16[7168,1024]{1,0:T(8,128)(2,1)} %param.6, bf16[1024,1024]{1,0:T(8,128)(2,1)} %get-tuple-element.22.refs_4_), kind=kOutput, calls=%fused_computation.32 | convolution fusion | flops 940900352 | bytes 6029312 | tf_op jit(solution)/shard_map/dot_general | solution.py:151
  109.2 3.4 %add_convert_fusion.1 = bf16[256,1792]{1,0:T(8,128)(2,1)S(1)} fusion(bf16[512,1792]{1,0:T(8,128)(2,1)} %collective-permute-done.6.refs_1_, bf16[7168,1024]{1,0:T(8,128)(2,1)} %param.6, bf16[1024,1024]{1,0:T(8,128)(2,1)S(1)} %copy-done), kind=kOutput, calls=%fused_computation.33 | convolution fusion | flops 940900352 | bytes 6029312 | tf_op jit(solution)/shard_map/dot_general | solution.py:151
  113.2 1.9 constant_dynamic-update-slice_fusion.7
  116.9 19.8 %collective-permute-done.10.refs_2_ = bf16[256,1792]{1,0:T(8,128)(2,1)S(1)} collective-permute-done((bf16[256,1792]{1,0:T(8,128)(2,1)S(1)}, bf16[256,1792]{1,0:T(8,128)(2,1)S(1)}, u32[]{:S(2)}, u32[]{:S(2)}) %collective-permute-start.10) | collective-permute-done | bytes 917536 | tf_op jit(solution)/shard_map/ppermute | solution.py:17
  141.4 5.3 %collective-permute-done.11.refs_3_ = bf16[128,1792]{1,0:T(8,128)(2,1)S(1)} collective-permute-done((bf16[128,1792]{1,0:T(8,128)(2,1)S(1)}, bf16[128,1792]{1,0:T(8,128)(2,1)S(1)}, u32[]{:S(2)}, u32[]{:S(2)}) %collective-permute-start.11) | collective-permute-done | bytes 458784 | tf_op jit(solution)/shard_map/ppermute | solution.py:17
  147.5 3.6 %adam.6 = (bf16[1792,128]{1,0:T(8,128)(2,1)}, f32[128,7168]{1,0:T(8,128)}, f32[128,7168]{1,0:T(8,128)}) custom-call(bf16[256,1792]{1,0:T(8,128)(2,1)} %fusion.35.refs_0_, bf16[512,1792]{1,0:T(8,128)(2,1)} %collective-permute-done.9.refs_1_, bf16[256,1792]{1,0:T(8,128)(2,1)} %copy-done.14, ...), custom_call_target="tpu_custom_call", output_to_operand_aliasing={{1}: (6, {}), {2}: (7, {})} | custom-call | flops 4587520 | bytes 5505024 | tf_op jit(solution)/shard_map/adam/pallas_call | solution.py:104
  154.5 2.0 collective-permute-done.29.refs_2_
  156.5 7.2 %collective-permute-done.8.refs_3_ = bf16[128,1792]{1,0:T(8,128)(2,1)S(1)} collective-permute-done((bf16[128,1792]{1,0:T(8,128)(2,1)S(1)}, bf16[128,1792]{1,0:T(8,128)(2,1)S(1)}, u32[]{:S(2)}, u32[]{:S(2)}) %collective-permute-start.8) | collective-permute-done | bytes 458784 | tf_op jit(solution)/shard_map/ppermute | solution.py:17
  164.5 3.6 %adam.7 = (bf16[1792,128]{1,0:T(8,128)(2,1)}, f32[128,7168]{1,0:T(8,128)}, f32[128,7168]{1,0:T(8,128)}) custom-call(bf16[256,1792]{1,0:T(8,128)(2,1)} %copy-done.8, bf16[512,1792]{1,0:T(8,128)(2,1)} %collective-permute-done.6.refs_1_, bf16[256,1792]{1,0:T(8,128)(2,1)} %copy-done.10, ...), custom_call_target="tpu_custom_call", output_to_operand_aliasing={{1}: (6, {}), {2}: (7, {})} | custom-call | flops 4587520 | bytes 5505024 | tf_op jit(solution)/shard_map/adam/pallas_call | solution.py:104
  169.0 11.5 %collective-permute-done.16 = bf16[1792,128]{1,0:T(8,128)(2,1)S(1)} collective-permute-done((bf16[1792,128]{1,0:T(8,128)(2,1)}, bf16[1792,128]{1,0:T(8,128)(2,1)S(1)}, u32[]{:S(2)}, u32[]{:S(2)}) %collective-permute-start.16) | collective-permute-done | bytes 458784 | tf_op jit(solution)/shard_map/ppermute | solution.py:17
  183.4 18.3 %collective-permute-done.21.refs_2_ = bf16[1792,256]{1,0:T(8,128)(2,1)} collective-permute-done((bf16[1792,256]{1,0:T(8,128)(2,1)S(1)}, bf16[1792,256]{1,0:T(8,128)(2,1)}, u32[]{:S(2)}, u32[]{:S(2)}) %collective-permute-start.21) | collective-permute-done | bytes 917536 | tf_op jit(solution)/shard_map/ppermute | solution.py:17
  203.4 8.7 %back.4.refs_5_ = f32[7168,1024]{1,0:T(8,128)} custom-call(bf16[1792,256]{1,0:T(8,128)(2,1)} %collective-permute-done.30.refs_0_, bf16[1792,256]{1,0:T(8,128)(2,1)} %collective-permute-done.31.refs_1_, bf16[1792,256]{1,0:T(8,128)(2,1)} %collective-permute-done.29.refs_2_, bf16[1792,256]{1,0:T(8,128)(2,1)} %constant_dynamic-update-slice_fusion.6.refs_3_, ...), custom_call_target="tpu_custom_call" | custom-call | flops 3758096384 | bytes 11010048 | tf_op jit(solution)/shard_map/back/pallas_call | solution.py:135
  212.1 8.7 %back.5.refs_5_ = f32[7168,1024]{1,0:T(8,128)} custom-call(bf16[1792,256]{1,0:T(8,128)(2,1)} %collective-permute-done.26.refs_0_, bf16[1792,256]{1,0:T(8,128)(2,1)} %collective-permute-done.27.refs_1_, bf16[1792,256]{1,0:T(8,128)(2,1)} %collective-permute-done.25.refs_2_, bf16[1792,256]{1,0:T(8,128)(2,1)} %copy-done.5, ...), custom_call_target="tpu_custom_call", output_to_operand_aliasing={{}: (5, {})} | custom-call | flops 3758096384 | bytes 11010048 | tf_op jit(solution)/shard_map/back/pallas_call | solution.py:135
  221.8 8.7 %back.6.refs_5_ = f32[7168,1024]{1,0:T(8,128)} custom-call(bf16[1792,256]{1,0:T(8,128)(2,1)} %collective-permute-done.22.refs_0_, bf16[1792,256]{1,0:T(8,128)(2,1)} %copy-done.18, bf16[1792,256]{1,0:T(8,128)(2,1)} %collective-permute-done.21.refs_2_, bf16[1792,256]{1,0:T(8,128)(2,1)} %copy-done.6, ...), custom_call_target="tpu_custom_call", output_to_operand_aliasing={{}: (5, {})} | custom-call | flops 3758096384 | bytes 11010048 | tf_op jit(solution)/shard_map/back/pallas_call | solution.py:135
  230.5 8.7 %back.7 = f32[7168,1024]{1,0:T(8,128)} custom-call(bf16[1792,256]{1,0:T(8,128)(2,1)} %collective-permute-done.18.refs_0_, bf16[1792,256]{1,0:T(8,128)(2,1)} %collective-permute-done.19.refs_1_, bf16[1792,256]{1,0:T(8,128)(2,1)} %collective-permute-done.17.refs_2_, bf16[1792,256]{1,0:T(8,128)(2,1)} %copy-done.7, ...), custom_call_target="tpu_custom_call", output_to_operand_aliasing={{}: (5, {})} | custom-call | flops 3758096384 | bytes 11010048 | tf_op jit(solution)/shard_map/back/pallas_call | solution.py:135
  (121 shorter events, 39.4 us)
Async XLA Ops:
  1.9 17.9 %collective-permute-start = (bf16[256,1024]{1,0:T(8,128)(2,1)S(1)}, bf16[256,1024]{1,0:T(8,128)(2,1)S(1)}, u32[]{:S(2)}, u32[]{:S(2)}) collective-permute-start(bf16[256,1024]{1,0:T(8,128)(2,1)S(1)} %bitcast.5), channel_id=1, source_target_pairs={{0,8},{8,16},{16,24},{24,0},{1,9},{9,17},{17,25},{25,1},{2,10},{10... | collective-permute-start | bytes 1572872 | tf_op jit(solution)/shard_map/ppermute | solution.py:21
  5.0 24.9 %collective-permute-start.2 = (bf16[256,1024]{1,0:T(8,128)(2,1)S(1)}, bf16[256,1024]{1,0:T(8,128)(2,1)S(1)}, u32[]{:S(2)}, u32[]{:S(2)}) collective-permute-start(bf16[256,1024]{1,0:T(8,128)(2,1)S(1)} %bitcast.6), channel_id=1, source_target_pairs={{0,24},{8,0},{16,8},{24,16},{1,25},{9,1},{17,9},{25,17},{2,26},{10... | collective-permute-start | bytes 1572872 | tf_op jit(solution)/shard_map/ppermute | solution.py:21
  19.9 18.6 %collective-permute-start.1 = (bf16[128,1024]{1,0:T(8,128)(2,1)S(1)}, bf16[128,1024]{1,0:T(8,128)(2,1)S(1)}, u32[]{:S(2)}, u32[]{:S(2)}) collective-permute-start(bf16[128,1024]{1,0:T(8,128)(2,1)S(1)} %slice.136), channel_id=1, source_target_pairs={{0,8},{8,16},{16,24},{24,0},{1,9},{9,17},{17,25},{25,1},{2,10},{10... | collective-permute-start | bytes 786440 | tf_op jit(solution)/shard_map/ppermute | solution.py:21
  29.9 11.6 %collective-permute-start.3 = (bf16[128,1024]{1,0:T(8,128)(2,1)S(1)}, bf16[128,1024]{1,0:T(8,128)(2,1)S(1)}, u32[]{:S(2)}, u32[]{:S(2)}) collective-permute-start(bf16[128,1024]{1,0:T(8,128)(2,1)S(1)} %slice.137), channel_id=1, source_target_pairs={{0,24},{8,0},{16,8},{24,16},{1,25},{9,1},{17,9},{25,17},{2,26},{10... | collective-permute-start | bytes 786440 | tf_op jit(solution)/shard_map/ppermute | solution.py:21
  50.9 8.0 %collective-permute-start.4 = (bf16[512,1792]{1,0:T(8,128)(2,1)S(1)}, bf16[512,1792]{1,0:T(8,128)(2,1)S(1)}, u32[]{:S(2)}, u32[]{:S(2)}) collective-permute-start(bf16[512,1792]{1,0:T(8,128)(2,1)S(1)} %convolution_convert_fusion.3), channel_id=1, source_target_pairs={{0,1},{1,0},{2,3},{3,2},{4,5},{5,4},{6,7},{7,6},{8,9},{9,8},{10,11... | collective-permute-start | bytes 5505032 | tf_op jit(solution)/shard_map/ppermute | solution.py:17
  55.9 5.7 %collective-permute-start.5 = (bf16[512,1792]{1,0:T(8,128)(2,1)S(1)}, bf16[512,1792]{1,0:T(8,128)(2,1)S(1)}, u32[]{:S(2)}, u32[]{:S(2)}) collective-permute-start(bf16[512,1792]{1,0:T(8,128)(2,1)S(1)} %convolution_convert_fusion.2), channel_id=1, source_target_pairs={{0,1},{1,0},{2,3},{3,2},{4,5},{5,4},{6,7},{7,6},{8,9},{9,8},{10,11... | collective-permute-start | bytes 5505032 | tf_op jit(solution)/shard_map/ppermute | solution.py:17
  60.0 22.3 %collective-permute-start.14 = (bf16[256,1792]{1,0:T(8,128)(2,1)S(1)}, bf16[256,1792]{1,0:T(8,128)(2,1)S(1)}, u32[]{:S(2)}, u32[]{:S(2)}) collective-permute-start(bf16[256,1792]{1,0:T(8,128)(2,1)S(1)} %fusion.41), channel_id=1, source_target_pairs={{0,2},{1,3},{2,0},{3,1},{4,6},{5,7},{6,4},{7,5},{8,10},{9,11},{10,... | collective-permute-start | bytes 2752520 | tf_op jit(solution)/shard_map/ppermute | solution.py:17
  62.7 22.5 %collective-permute-start.12 = (bf16[256,1792]{1,0:T(8,128)(2,1)S(1)}, bf16[256,1792]{1,0:T(8,128)(2,1)S(1)}, u32[]{:S(2)}, u32[]{:S(2)}) collective-permute-start(bf16[256,1792]{1,0:T(8,128)(2,1)S(1)} %fusion.38), channel_id=1, source_target_pairs={{0,4},{1,5},{2,6},{3,7},{4,0},{5,1},{6,2},{7,3},{8,12},{9,13},{10,... | collective-permute-start | bytes 2752520 | tf_op jit(solution)/shard_map/ppermute | solution.py:17
  67.7 36.8 %collective-permute-start.9 = (bf16[512,1792]{1,0:T(8,128)(2,1)}, bf16[512,1792]{1,0:T(8,128)(2,1)}, u32[]{:S(2)}, u32[]{:S(2)}) collective-permute-start(bf16[512,1792]{1,0:T(8,128)(2,1)} %convolution_convert_fusion), channel_id=1, source_target_pairs={{0,1},{1,0},{2,3},{3,2},{4,5},{5,4},{6,7},{7,6},{8,9},{9,8},{10,11... | collective-permute-start | bytes 5505032 | tf_op jit(solution)/shard_map/ppermute | solution.py:17
  71.0 38.1 %collective-permute-start.6 = (bf16[512,1792]{1,0:T(8,128)(2,1)}, bf16[512,1792]{1,0:T(8,128)(2,1)}, u32[]{:S(2)}, u32[]{:S(2)}) collective-permute-start(bf16[512,1792]{1,0:T(8,128)(2,1)} %convolution_convert_fusion.1), channel_id=1, source_target_pairs={{0,1},{1,0},{2,3},{3,2},{4,5},{5,4},{6,7},{7,6},{8,9},{9,8},{10,11... | collective-permute-start | bytes 5505032 | tf_op jit(solution)/shard_map/ppermute | solution.py:17
  82.5 12.2 %collective-permute-start.15 = (bf16[128,1792]{1,0:T(8,128)(2,1)S(1)}, bf16[128,1792]{1,0:T(8,128)(2,1)}, u32[]{:S(2)}, u32[]{:S(2)}) collective-permute-start(bf16[128,1792]{1,0:T(8,128)(2,1)S(1)} %add_convert_fusion.2), channel_id=1, source_target_pairs={{0,4},{1,5},{2,6},{3,7},{4,0},{5,1},{6,2},{7,3},{8,12},{9,13},{10,... | collective-permute-start | bytes 1376264 | tf_op jit(solution)/shard_map/ppermute | solution.py:17
  85.4 14.4 %collective-permute-start.13 = (bf16[128,1792]{1,0:T(8,128)(2,1)S(1)}, bf16[128,1792]{1,0:T(8,128)(2,1)}, u32[]{:S(2)}, u32[]{:S(2)}) collective-permute-start(bf16[128,1792]{1,0:T(8,128)(2,1)S(1)} %add_convert_fusion.3), channel_id=1, source_target_pairs={{0,2},{1,3},{2,0},{3,1},{4,6},{5,7},{6,4},{7,5},{8,10},{9,11},{10,... | collective-permute-start | bytes 1376264 | tf_op jit(solution)/shard_map/ppermute | solution.py:17
  98.3 14.9 %collective-permute-start.28 = (bf16[1792,128]{1,0:T(8,128)(2,1)}, bf16[1792,128]{1,0:T(8,128)(2,1)}, u32[]{:S(2)}, u32[]{:S(2)}) collective-permute-start(bf16[1792,128]{1,0:T(8,128)(2,1)} %get-tuple-element.32), channel_id=1, source_target_pairs={{0,4},{1,5},{2,6},{3,7},{4,0},{5,1},{6,2},{7,3},{8,12},{9,13},{10,... | collective-permute-start | bytes 1376264 | tf_op jit(solution)/shard_map/ppermute | solution.py:17
  103.4 48.3 %collective-permute-start.24 = (bf16[1792,128]{1,0:T(8,128)(2,1)}, bf16[1792,128]{1,0:T(8,128)(2,1)}, u32[]{:S(2)}, u32[]{:S(2)}) collective-permute-start(bf16[1792,128]{1,0:T(8,128)(2,1)} %get-tuple-element.31), channel_id=1, source_target_pairs={{0,2},{1,3},{2,0},{3,1},{4,6},{5,7},{6,4},{7,5},{8,10},{9,11},{10,... | collective-permute-start | bytes 1376264 | tf_op jit(solution)/shard_map/ppermute | solution.py:17
  108.1 28.6 %collective-permute-start.10 = (bf16[256,1792]{1,0:T(8,128)(2,1)S(1)}, bf16[256,1792]{1,0:T(8,128)(2,1)S(1)}, u32[]{:S(2)}, u32[]{:S(2)}) collective-permute-start(bf16[256,1792]{1,0:T(8,128)(2,1)S(1)} %add_convert_fusion), channel_id=1, source_target_pairs={{0,2},{1,3},{2,0},{3,1},{4,6},{5,7},{6,4},{7,5},{8,10},{9,11},{10,... | collective-permute-start | bytes 2752520 | tf_op jit(solution)/shard_map/ppermute | solution.py:17
  112.6 26.2 %collective-permute-start.7 = (bf16[256,1792]{1,0:T(8,128)(2,1)S(1)}, bf16[256,1792]{1,0:T(8,128)(2,1)S(1)}, u32[]{:S(2)}, u32[]{:S(2)}) collective-permute-start(bf16[256,1792]{1,0:T(8,128)(2,1)S(1)} %add_convert_fusion.1), channel_id=1, source_target_pairs={{0,4},{1,5},{2,6},{3,7},{4,0},{5,1},{6,2},{7,3},{8,12},{9,13},{10,... | collective-permute-start | bytes 2752520 | tf_op jit(solution)/shard_map/ppermute | solution.py:17
  115.9 40.6 %collective-permute-start.29 = (bf16[1792,256]{1,0:T(8,128)(2,1)}, bf16[1792,256]{1,0:T(8,128)(2,1)}, u32[]{:S(2)}, u32[]{:S(2)}) collective-permute-start(bf16[1792,256]{1,0:T(8,128)(2,1)} %constant_dynamic-update-slice_fusion.6.refs_3_), channel_id=1, source_target_pairs={{0,2},{1,3},{2,0},{3,1},{4,6},{5,7},{6,4},{7,5},{8,10},{9,11},{10,... | collective-permute-start | bytes 2752520 | tf_op jit(solution)/shard_map/ppermute | solution.py:17
  116.9 65.4 %collective-permute-start.31 = (bf16[1792,256]{1,0:T(8,128)(2,1)}, bf16[1792,256]{1,0:T(8,128)(2,1)}, u32[]{:S(2)}, u32[]{:S(2)}) collective-permute-start(bf16[1792,256]{1,0:T(8,128)(2,1)} %constant_dynamic-update-slice_fusion.6.refs_3_), channel_id=1, source_target_pairs={{0,1},{1,0},{2,3},{3,2},{4,5},{5,4},{6,7},{7,6},{8,9},{9,8},{10,11... | collective-permute-start | bytes 2752520 | tf_op jit(solution)/shard_map/ppermute | solution.py:17
  138.2 8.5 %collective-permute-start.11 = (bf16[128,1792]{1,0:T(8,128)(2,1)S(1)}, bf16[128,1792]{1,0:T(8,128)(2,1)S(1)}, u32[]{:S(2)}, u32[]{:S(2)}) collective-permute-start(bf16[128,1792]{1,0:T(8,128)(2,1)S(1)} %add_convert_fusion.4), channel_id=1, source_target_pairs={{0,4},{1,5},{2,6},{3,7},{4,0},{5,1},{6,2},{7,3},{8,12},{9,13},{10,... | collective-permute-start | bytes 1376264 | tf_op jit(solution)/shard_map/ppermute | solution.py:17
  140.3 23.4 %collective-permute-start.8 = (bf16[128,1792]{1,0:T(8,128)(2,1)S(1)}, bf16[128,1792]{1,0:T(8,128)(2,1)S(1)}, u32[]{:S(2)}, u32[]{:S(2)}) collective-permute-start(bf16[128,1792]{1,0:T(8,128)(2,1)S(1)} %add_convert_fusion.5), channel_id=1, source_target_pairs={{0,2},{1,3},{2,0},{3,1},{4,6},{5,7},{6,4},{7,5},{8,10},{9,11},{10,... | collective-permute-start | bytes 1376264 | tf_op jit(solution)/shard_map/ppermute | solution.py:17
  151.1 16.9 %collective-permute-start.20 = (bf16[1792,128]{1,0:T(8,128)(2,1)}, bf16[1792,128]{1,0:T(8,128)(2,1)S(1)}, u32[]{:S(2)}, u32[]{:S(2)}) collective-permute-start(bf16[1792,128]{1,0:T(8,128)(2,1)} %get-tuple-element.30), channel_id=1, source_target_pairs={{0,4},{1,5},{2,6},{3,7},{4,0},{5,1},{6,2},{7,3},{8,12},{9,13},{10,... | collective-permute-start | bytes 1376264 | tf_op jit(solution)/shard_map/ppermute | solution.py:17
  152.9 30.0 %collective-permute-start.25 = (bf16[1792,256]{1,0:T(8,128)(2,1)S(1)}, bf16[1792,256]{1,0:T(8,128)(2,1)}, u32[]{:S(2)}, u32[]{:S(2)}) collective-permute-start(bf16[1792,256]{1,0:T(8,128)(2,1)S(1)} %constant_dynamic-update-slice_fusion.4.refs_3_), channel_id=1, source_target_pairs={{0,4},{1,5},{2,6},{3,7},{4,0},{5,1},{6,2},{7,3},{8,12},{9,13},{10,... | collective-permute-start | bytes 2752520 | tf_op jit(solution)/shard_map/ppermute | solution.py:17
  156.5 26.5 %collective-permute-start.27 = (bf16[1792,256]{1,0:T(8,128)(2,1)S(1)}, bf16[1792,256]{1,0:T(8,128)(2,1)}, u32[]{:S(2)}, u32[]{:S(2)}) collective-permute-start(bf16[1792,256]{1,0:T(8,128)(2,1)S(1)} %constant_dynamic-update-slice_fusion.4.refs_3_), channel_id=1, source_target_pairs={{0,1},{1,0},{2,3},{3,2},{4,5},{5,4},{6,7},{7,6},{8,9},{9,8},{10,11... | collective-permute-start | bytes 2752520 | tf_op jit(solution)/shard_map/ppermute | solution.py:17
  163.7 38.1 %collective-permute-start.30 = (bf16[1792,256]{1,0:T(8,128)(2,1)}, bf16[1792,256]{1,0:T(8,128)(2,1)}, u32[]{:S(2)}, u32[]{:S(2)}) collective-permute-start(bf16[1792,256]{1,0:T(8,128)(2,1)} %collective-permute-done.29.refs_2_), channel_id=1, source_target_pairs={{0,1},{1,0},{2,3},{3,2},{4,5},{5,4},{6,7},{7,6},{8,9},{9,8},{10,11... | collective-permute-start | bytes 2752520 | tf_op jit(solution)/shard_map/ppermute | solution.py:17
  168.1 12.5 %collective-permute-start.16 = (bf16[1792,128]{1,0:T(8,128)(2,1)}, bf16[1792,128]{1,0:T(8,128)(2,1)S(1)}, u32[]{:S(2)}, u32[]{:S(2)}) collective-permute-start(bf16[1792,128]{1,0:T(8,128)(2,1)} %get-tuple-element.29), channel_id=1, source_target_pairs={{0,2},{1,3},{2,0},{3,1},{4,6},{5,7},{6,4},{7,5},{8,10},{9,11},{10,... | collective-permute-start | bytes 1376264 | tf_op jit(solution)/shard_map/ppermute | solution.py:17
  180.5 21.3 %collective-permute-start.21 = (bf16[1792,256]{1,0:T(8,128)(2,1)S(1)}, bf16[1792,256]{1,0:T(8,128)(2,1)}, u32[]{:S(2)}, u32[]{:S(2)}) collective-permute-start(bf16[1792,256]{1,0:T(8,128)(2,1)S(1)} %constant_dynamic-update-slice_fusion.2.refs_3_), channel_id=1, source_target_pairs={{0,2},{1,3},{2,0},{3,1},{4,6},{5,7},{6,4},{7,5},{8,10},{9,11},{10,... | collective-permute-start | bytes 2752520 | tf_op jit(solution)/shard_map/ppermute | solution.py:17
  182.4 21.0 %collective-permute-start.17 = (bf16[1792,256]{1,0:T(8,128)(2,1)S(1)}, bf16[1792,256]{1,0:T(8,128)(2,1)}, u32[]{:S(2)}, u32[]{:S(2)}) collective-permute-start(bf16[1792,256]{1,0:T(8,128)(2,1)S(1)} %constant_dynamic-update-slice_fusion.refs_3_), channel_id=1, source_target_pairs={{0,4},{1,5},{2,6},{3,7},{4,0},{5,1},{6,2},{7,3},{8,12},{9,13},{10,... | collective-permute-start | bytes 2752520 | tf_op jit(solution)/shard_map/ppermute | solution.py:17
  182.9 29.2 %collective-permute-start.26 = (bf16[1792,256]{1,0:T(8,128)(2,1)}, bf16[1792,256]{1,0:T(8,128)(2,1)}, u32[]{:S(2)}, u32[]{:S(2)}) collective-permute-start(bf16[1792,256]{1,0:T(8,128)(2,1)} %collective-permute-done.25.refs_2_), channel_id=1, source_target_pairs={{0,1},{1,0},{2,3},{3,2},{4,5},{5,4},{6,7},{7,6},{8,9},{9,8},{10,11... | collective-permute-start | bytes 2752520 | tf_op jit(solution)/shard_map/ppermute | solution.py:17
  182.9 37.9 %collective-permute-start.23 = (bf16[1792,256]{1,0:T(8,128)(2,1)S(1)}, bf16[1792,256]{1,0:T(8,128)(2,1)S(1)}, u32[]{:S(2)}, u32[]{:S(2)}) collective-permute-start(bf16[1792,256]{1,0:T(8,128)(2,1)S(1)} %constant_dynamic-update-slice_fusion.2.refs_3_), channel_id=1, source_target_pairs={{0,1},{1,0},{2,3},{3,2},{4,5},{5,4},{6,7},{7,6},{8,9},{9,8},{10,11... | collective-permute-start | bytes 2752520 | tf_op jit(solution)/shard_map/ppermute | solution.py:17
  201.8 19.1 %collective-permute-start.22 = (bf16[1792,256]{1,0:T(8,128)(2,1)}, bf16[1792,256]{1,0:T(8,128)(2,1)}, u32[]{:S(2)}, u32[]{:S(2)}) collective-permute-start(bf16[1792,256]{1,0:T(8,128)(2,1)} %collective-permute-done.21.refs_2_), channel_id=1, source_target_pairs={{0,1},{1,0},{2,3},{3,2},{4,5},{5,4},{6,7},{7,6},{8,9},{9,8},{10,11... | collective-permute-start | bytes 2752520 | tf_op jit(solution)/shard_map/ppermute | solution.py:17
  201.8 28.7 %collective-permute-start.19 = (bf16[1792,256]{1,0:T(8,128)(2,1)S(1)}, bf16[1792,256]{1,0:T(8,128)(2,1)}, u32[]{:S(2)}, u32[]{:S(2)}) collective-permute-start(bf16[1792,256]{1,0:T(8,128)(2,1)S(1)} %constant_dynamic-update-slice_fusion.refs_3_), channel_id=1, source_target_pairs={{0,1},{1,0},{2,3},{3,2},{4,5},{5,4},{6,7},{7,6},{8,9},{9,8},{10,11... | collective-permute-start | bytes 2752520 | tf_op jit(solution)/shard_map/ppermute | solution.py:17
  203.4 27.1 %collective-permute-start.18 = (bf16[1792,256]{1,0:T(8,128)(2,1)}, bf16[1792,256]{1,0:T(8,128)(2,1)}, u32[]{:S(2)}, u32[]{:S(2)}) collective-permute-start(bf16[1792,256]{1,0:T(8,128)(2,1)} %collective-permute-done.17.refs_2_), channel_id=1, source_target_pairs={{0,1},{1,0},{2,3},{3,2},{4,5},{5,4},{6,7},{7,6},{8,9},{9,8},{10,11... | collective-permute-start | bytes 2752520 | tf_op jit(solution)/shard_map/ppermute | solution.py:17
  (25 other events, 403.9 us)
